TPU v7x, 32 devices: a whole 2x2x4 slice. The times are simulated.
32 devices in a mesh: dp: 8 (over z, y), tensor: 4 (over x, core).
Axes of the slice: x: 2, y: 2, z: 4, core: 2. Of those that a mesh axis runs over, the one named last changes fastest.
Arguments:
- block_input: bfloat16 [8192, 1536], P(('dp', 'tensor')), may hold values from -6 to 6
- segment_ids: int32 [8, 1024], P('dp'), may hold values from 0 to 3, as said below
- gain_attn: float32 [1536], replicated, may hold values from 0.5 to 1.5
- w_query: bfloat16 [1536, 1536], P('dp', 'tensor'), may hold values from -0.15625 to 0.15625
- b_query: float32 [1536], P('tensor'), may hold values from -3 to 3
- w_keyval: bfloat16 [1536, 512], P('dp'), may hold values from -0.15625 to 0.15625
- b_keyval: float32 [512], replicated, may hold values from -3 to 3
- w_out: bfloat16 [1536, 1536], P('tensor', 'dp'), may hold values from -0.625 to 0.625
- gain_ffn: float32 [1536], replicated, may hold values from 0.5 to 1.5
- w_gate: bfloat16 [1536, 8960], P('dp', 'tensor'), may hold values from -0.15625 to 0.15625
- w_up: bfloat16 [1536, 8960], P('dp', 'tensor'), may hold values from -0.15625 to 0.15625
- w_down: bfloat16 [8960, 1536], P('tensor', 'dp'), may hold values from -0.0625 to 0.0625
- cotangent: bfloat16 [8192, 1536], P(('dp', 'tensor')), may hold values from -6 to 6
Outputs:
- block_output: bfloat16 [8192, 1536], P(('dp', 'tensor'))
- grad_input: bfloat16 [8192, 1536], P(('dp', 'tensor'))
- grad_gain_attn: float32 [1536], P(('dp', 'tensor'))
- grad_w_query: float32 [1536, 1536], P('dp', 'tensor')
- grad_b_query: float32 [1536], P(('dp', 'tensor'))
- grad_w_keyval: float32 [1536, 512], P(('dp', 'tensor'))
- grad_b_keyval: float32 [512], P(('dp', 'tensor'))
- grad_w_out: float32 [1536, 1536], P('tensor', 'dp')
- grad_gain_ffn: float32 [1536], P(('dp', 'tensor'))
- grad_w_gate: float32 [1536, 8960], P('dp', 'tensor')
- grad_w_up: float32 [1536, 8960], P('dp', 'tensor')
- grad_w_down: float32 [8960, 1536], P('tensor', 'dp')
Inputs may be any that keep to these rules, and one draw needn't show every extreme that they name: `segment_ids`: ids start at 0 and never fall along a sequence, each rising by one at a document's start; a sequence holds 2 to 4 documents, each of 204 tokens or more; some sequence holds 4.
All inputs are finite; a program needn't handle non-finite values.
Results may differ from a plain program's by a relative error of at most 0.018.
Values may be sent and summed in bfloat16 or wider, within the bound.
No kernel may reach another device: no remote copies, remote signals or barrier semaphores. Data moves between devices by JAX's collectives and lax.ppermute only.
A program may use at most 256 MiB of HBM per device.

v0:
```python
import math
import jax
import jax.numpy as jnp
from jax import lax
from jax.sharding import PartitionSpec as P

HQ = 12
KV = 2
HD = 128
epsilon = 1e-06
rope_base = 1000000.0
masked_score = -1e30


def matmul(left, right):
    return jnp.dot(left, right, preferred_element_type=jnp.float32)


def positions_of(segment_row):
    index_row = jnp.arange(segment_row.shape[0], dtype=jnp.int32)
    starts = jnp.concatenate(
        [jnp.ones((1,), jnp.int32), (segment_row[1:] != segment_row[:-1]).astype(jnp.int32)]
    )
    first_index = lax.cummax(jnp.where(starts > 0, index_row, 0), axis=0)
    return index_row - first_index


def allowed_of(segment_row):
    index_row = jnp.arange(segment_row.shape[0], dtype=jnp.int32)
    causal = index_row[:, None] >= index_row[None, :]
    return causal & (segment_row[:, None] == segment_row[None, :])


def rotary(positions):
    inverse = rope_base ** (-(jnp.arange(HD // 2, dtype=jnp.float32) * 2.0 / HD))
    angles = positions.astype(jnp.float32)[:, None] * inverse[None, :]
    angles = jnp.concatenate([angles, angles], axis=1)
    return (jnp.cos(angles), jnp.sin(angles))


def turn(values_in, cosine_table, sine_table):
    half_size = values_in.shape[-1] // 2
    rolled = jnp.concatenate([-values_in[..., half_size:], values_in[..., :half_size]], axis=-1)
    return values_in * cosine_table + rolled * sine_table


def norm_forward(values_in):
    row_scale = lax.rsqrt(jnp.mean(values_in * values_in, axis=-1, keepdims=True) + epsilon)
    return (values_in * row_scale, row_scale)


def norm_backward(grad_out, normed, row_scale, gain_vec):
    grad_normed = grad_out * gain_vec
    grad_in = row_scale * (
        grad_normed - normed * jnp.mean(grad_normed * normed, axis=-1, keepdims=True)
    )
    return (grad_in, jnp.sum(grad_out * normed, axis=0))


def gather_three(first, second, third):
    return (
        lax.all_gather(first, "dp", axis=0, tiled=True),
        lax.all_gather(second, "dp", axis=0, tiled=True),
        lax.all_gather(third, "dp", axis=1, tiled=True),
    )


def masked_scores(query_rot, key_rot, segment_row):
    raw_scores = jnp.einsum(
        "qhd,kd->hqk", query_rot, key_rot, preferred_element_type=jnp.float32
    ) / math.sqrt(HD)
    return jnp.where(allowed_of(segment_row)[None], raw_scores, masked_score)


def attend(query_rot, key_rot, value_rows, segment_row):
    scores = masked_scores(query_rot, key_rot, segment_row)
    row_max = jnp.max(scores, axis=2, keepdims=True)
    log_total = row_max + jnp.log(jnp.sum(jnp.exp(scores - row_max), axis=2, keepdims=True))
    probs_low = jnp.exp(scores - log_total).astype(jnp.bfloat16)
    attn_result = jnp.einsum(
        "hqk,kd->qhd", probs_low, value_rows, preferred_element_type=jnp.float32
    )
    return (attn_result, log_total)


def attend_back(query_rot, key_rot, value_rows, segment_row, log_total, attn_result, grad_context):
    scores = masked_scores(query_rot, key_rot, segment_row)
    attn_probs = jnp.exp(scores - log_total)
    probs_low = attn_probs.astype(jnp.bfloat16)
    grad_probs = jnp.einsum(
        "qhd,kd->hqk", grad_context, value_rows, preferred_element_type=jnp.float32
    )
    row_delta = jnp.sum(grad_context.astype(jnp.float32) * attn_result, axis=2).T[:, :, None]
    grad_scores = (attn_probs * (grad_probs - row_delta)).astype(jnp.bfloat16)
    grad_query_rot = jnp.einsum(
        "hqk,kd->qhd", grad_scores, key_rot, preferred_element_type=jnp.float32
    ) / math.sqrt(HD)
    grad_key_rot = jnp.einsum(
        "hqk,qhd->kd", grad_scores, query_rot, preferred_element_type=jnp.float32
    ) / math.sqrt(HD)
    grad_value = jnp.einsum(
        "hqk,qhd->kd", probs_low, grad_context, preferred_element_type=jnp.float32
    )
    return (grad_query_rot, grad_key_rot, grad_value)


def local(
    block_input,
    segment_ids,
    gain_attn,
    w_query,
    b_query,
    w_keyval,
    b_keyval,
    w_out,
    gain_ffn,
    w_gate,
    w_up,
    w_down,
    cotangent,
):
    tensor_index = lax.axis_index("tensor")
    seq_count = segment_ids.shape[0]
    seq_length = segment_ids.shape[1]
    row_count = seq_count * seq_length
    local_heads = b_query.shape[0] // HD
    head_kv = tensor_index * local_heads // (HQ // KV)
    rows_float = block_input.astype(jnp.float32)
    normed_one, scale_one = norm_forward(rows_float)
    act_one = lax.all_gather(
        (normed_one * gain_attn).astype(jnp.bfloat16), "tensor", axis=0, tiled=True
    )
    query_w, keyval_w, out_w = gather_three(w_query, w_keyval, w_out)
    query_rows = matmul(act_one, query_w) + b_query
    keyval = matmul(act_one, keyval_w) + b_keyval
    key_rows = lax.dynamic_slice_in_dim(keyval, head_kv * HD, HD, 1)
    value_rows = lax.dynamic_slice_in_dim(keyval, KV * HD + head_kv * HD, HD, 1).astype(
        jnp.bfloat16
    )
    positions = jax.vmap(positions_of)(segment_ids).reshape(row_count)
    cosine_table, sine_table = rotary(positions)
    cos_heads = cosine_table[:, None, :]
    sin_heads = sine_table[:, None, :]
    query_rot = turn(query_rows.reshape(row_count, local_heads, HD), cos_heads, sin_heads).astype(
        jnp.bfloat16
    )
    key_rot = turn(key_rows, cosine_table, sine_table).astype(jnp.bfloat16)
    query_seq = query_rot.reshape(seq_count, seq_length, local_heads, HD)
    key_seq = key_rot.reshape(seq_count, seq_length, HD)
    value_seq = value_rows.reshape(seq_count, seq_length, HD)
    attn_result, log_total = lax.map(
        lambda seq_items: attend(*seq_items), (query_seq, key_seq, value_seq, segment_ids)
    )
    context = attn_result.astype(jnp.bfloat16).reshape(row_count, local_heads * HD)
    hidden = rows_float + lax.psum_scatter(
        matmul(context, out_w), "tensor", scatter_dimension=0, tiled=True
    )
    normed_two, scale_two = norm_forward(hidden)
    act_two = lax.all_gather(
        (normed_two * gain_ffn).astype(jnp.bfloat16), "tensor", axis=0, tiled=True
    )
    gate_w, up_w, down_w = gather_three(w_gate, w_up, w_down)
    gate_pre = matmul(act_two, gate_w)
    up_part = matmul(act_two, up_w)
    sigmoid_gate = jax.nn.sigmoid(gate_pre)
    silu_gate = gate_pre * sigmoid_gate
    mixed_rows = (silu_gate * up_part).astype(jnp.bfloat16)
    block_out = (
        hidden
        + lax.psum_scatter(
            matmul(mixed_rows, down_w).astype(jnp.bfloat16),
            "tensor",
            scatter_dimension=0,
            tiled=True,
        ).astype(jnp.float32)
    ).astype(jnp.bfloat16)
    cot_rows = lax.all_gather(cotangent, "tensor", axis=0, tiled=True)
    grad_mixed = matmul(cot_rows, down_w.T)
    grad_gate = (
        grad_mixed * up_part * sigmoid_gate * (1.0 + gate_pre * (1.0 - sigmoid_gate))
    ).astype(jnp.bfloat16)
    grad_up = (grad_mixed * silu_gate).astype(jnp.bfloat16)
    grad_gate_w = matmul(act_two.T, grad_gate)
    grad_up_w = matmul(act_two.T, grad_up)
    grad_down_w = matmul(mixed_rows.T, cot_rows)
    grad_act_two = lax.psum_scatter(
        matmul(grad_gate, gate_w.T) + matmul(grad_up, up_w.T),
        "tensor",
        scatter_dimension=0,
        tiled=True,
    )
    back_two, gain_two = norm_backward(grad_act_two, normed_two, scale_two, gain_ffn)
    grad_hidden = cotangent.astype(jnp.float32) + back_two
    grad_attn = lax.all_gather(grad_hidden.astype(jnp.bfloat16), "tensor", axis=0, tiled=True)
    grad_out_w = matmul(context.T, grad_attn)
    grad_context = (
        matmul(grad_attn, out_w.T)
        .astype(jnp.bfloat16)
        .reshape(seq_count, seq_length, local_heads, HD)
    )
    grad_query_rot, grad_key_rot, grad_value = lax.map(
        lambda seq_items: attend_back(*seq_items),
        (query_seq, key_seq, value_seq, segment_ids, log_total, attn_result, grad_context),
    )
    grad_query = turn(
        grad_query_rot.reshape(row_count, local_heads, HD), cos_heads, -sin_heads
    ).reshape(row_count, local_heads * HD)
    grad_key = turn(grad_key_rot.reshape(row_count, HD), cosine_table, -sine_table)
    grad_value = grad_value.reshape(row_count, HD)
    grad_query_low = grad_query.astype(jnp.bfloat16)
    kv_columns = jnp.zeros((row_count, keyval.shape[1]), jnp.bfloat16)
    kv_columns = lax.dynamic_update_slice_in_dim(
        kv_columns, grad_key.astype(jnp.bfloat16), head_kv * HD, 1
    )
    kv_columns = lax.dynamic_update_slice_in_dim(
        kv_columns, grad_value.astype(jnp.bfloat16), KV * HD + head_kv * HD, 1
    )
    bias_keyval = jnp.zeros((keyval.shape[1],), jnp.float32)
    bias_keyval = lax.dynamic_update_slice_in_dim(
        bias_keyval, jnp.sum(grad_key, axis=0), head_kv * HD, 0
    )
    bias_keyval = lax.dynamic_update_slice_in_dim(
        bias_keyval, jnp.sum(grad_value, axis=0), KV * HD + head_kv * HD, 0
    )
    bias_query = lax.dynamic_update_slice_in_dim(
        jnp.zeros((HQ * HD,), jnp.float32),
        jnp.sum(grad_query, axis=0),
        tensor_index * local_heads * HD,
        0,
    )
    grad_query_w = matmul(act_one.T, grad_query_low)
    grad_keyval_w = matmul(act_one.T, kv_columns)
    grad_act_one = lax.psum_scatter(
        (matmul(grad_query_low, query_w.T) + matmul(kv_columns, keyval_w.T)).astype(jnp.bfloat16),
        "tensor",
        scatter_dimension=0,
        tiled=True,
    ).astype(jnp.float32)
    back_one, gain_one = norm_backward(grad_act_one, normed_one, scale_one, gain_attn)
    grad_rows = (grad_hidden + back_one).astype(jnp.bfloat16)
    keyval_share, gain_one_share, gain_two_share, query_bias_share, keyval_bias_share = (
        lax.psum_scatter(grad_keyval_w, ("dp", "tensor"), scatter_dimension=0, tiled=True),
        lax.psum_scatter(gain_one, ("dp", "tensor"), scatter_dimension=0, tiled=True),
        lax.psum_scatter(gain_two, ("dp", "tensor"), scatter_dimension=0, tiled=True),
        lax.psum_scatter(bias_query, ("dp", "tensor"), scatter_dimension=0, tiled=True),
        lax.psum_scatter(bias_keyval, ("dp", "tensor"), scatter_dimension=0, tiled=True),
    )
    query_share, out_share, gate_share, up_share, down_share = (
        lax.psum_scatter(
            grad_query_w.astype(jnp.bfloat16), "dp", scatter_dimension=0, tiled=True
        ).astype(jnp.float32),
        lax.psum_scatter(
            grad_out_w.astype(jnp.bfloat16), "dp", scatter_dimension=1, tiled=True
        ).astype(jnp.float32),
        lax.psum_scatter(
            grad_gate_w.astype(jnp.bfloat16), "dp", scatter_dimension=0, tiled=True
        ).astype(jnp.float32),
        lax.psum_scatter(
            grad_up_w.astype(jnp.bfloat16), "dp", scatter_dimension=0, tiled=True
        ).astype(jnp.float32),
        lax.psum_scatter(
            grad_down_w.astype(jnp.bfloat16), "dp", scatter_dimension=1, tiled=True
        ).astype(jnp.float32),
    )
    return (
        block_out,
        grad_rows,
        gain_one_share,
        query_share,
        query_bias_share,
        keyval_share,
        keyval_bias_share,
        out_share,
        gain_two_share,
        gate_share,
        up_share,
        down_share,
    )


def solution(mesh):
    placed = (
        P(("dp", "tensor"), None),
        P("dp", None),
        P(),
        P("dp", "tensor"),
        P("tensor"),
        P("dp", None),
        P(),
        P("tensor", "dp"),
        P(),
        P("dp", "tensor"),
        P("dp", "tensor"),
        P("tensor", "dp"),
        P(("dp", "tensor"), None),
    )
    return jax.shard_map(
        local,
        mesh=mesh,
        in_specs=placed,
        out_specs=(
            P(("dp", "tensor"), None),
            P(("dp", "tensor"), None),
            P(("dp", "tensor")),
            P("dp", "tensor"),
            P(("dp", "tensor")),
            P(("dp", "tensor"), None),
            P(("dp", "tensor")),
            P("tensor", "dp"),
            P(("dp", "tensor")),
            P("dp", "tensor"),
            P("dp", "tensor"),
            P("tensor", "dp"),
        ),
        check_vma=False,
    )
```

profile of v0, /device:TPU:0, one launch (start us, length us, event | category | flops | bytes accessed | tf_op | source)
XLA Modules:
  0.0 1482.0 jit_solution(15097303568250098657)
XLA Ops:
  8.0 1.4 fusion.17
  9.4 2.3 fusion.14
  14.6 39.4 %all-gather.15.cloned.1.call-done = bf16[1536,384]{1,0:T(8,128)(2,1)} async-done(((bf16[192,384]{1,0:T(8,128)(2,1)}), bf16[1536,384]{1,0:T(8,128)(2,1)}) %all-gather.15.cloned.1.call-update) | async-done | bytes 1179664 | tf_op jit(solution)/shard_map/all_gather | solution.py:62
  54.0 29.5 %all-gather.11.cloned.1.call-done = bf16[1024,1536]{1,0:T(8,128)(2,1)} async-done(((bf16[256,1536]{1,0:T(8,128)(2,1)}), bf16[1024,1536]{1,0:T(8,128)(2,1)}) %all-gather.11.cloned.1.call-update) | async-done | bytes 3145744 | tf_op jit(solution)/shard_map/all_gather | solution.py:130
  83.5 3.6 convolution_add_fusion.2
  87.1 1.0 slice_negate_fusion.1
  88.2 41.7 %all-gather.13.cloned.1.call-done = bf16[1536,512]{1,0:T(8,128)(2,1)} async-done(((bf16[192,512]{1,0:T(8,128)(2,1)}), bf16[1536,512]{1,0:T(8,128)(2,1)}) %all-gather.13.cloned.1.call-update) | async-done | bytes 1572880 | tf_op jit(solution)/shard_map/all_gather | solution.py:63
  129.9 4.2 convolution_add_fusion.1
  134.9 3.4 broadcast_multiply_fusion
  138.9 6.0 fusion.4
  144.9 7.3 exponential_reduce_fusion
  152.2 9.5 bitcast_convert_fusion
  161.7 10.1 all-gather.17.cloned.1.call-done
  171.8 5.7 fusion.46
  178.2 56.6 %reduce-scatter.11.cloned.1.call-done = f32[256,1536]{1,0:T(8,128)} async-done(((f32[1024,1536]{1,0:T(8,128)}), f32[256,1536]{1,0:T(8,128)}) %reduce-scatter.11.cloned.1.call-update) | async-done | bytes 1572880 | tf_op jit(solution)/shard_map/reduce_scatter | solution.py:155
  234.8 1.7 multiply_reduce_fusion.2
  236.6 1.1 multiply_convert_fusion.3
  239.8 106.2 %all-gather.21.cloned.1.call-done = bf16[1536,2240]{1,0:T(8,128)(2,1)} async-done(((bf16[192,2240]{1,0:T(8,128)(2,1)}), bf16[1536,2240]{1,0:T(8,128)(2,1)}) %all-gather.21.cloned.1.call-update) | async-done | bytes 6881296 | tf_op jit(solution)/shard_map/all_gather | solution.py:62
  346.0 29.0 %all-gather.19.cloned.1.call-done = bf16[1024,1536]{1,0:T(8,128)(2,1)} async-done(((bf16[256,1536]{1,0:T(8,128)(2,1)}), bf16[1024,1536]{1,0:T(8,128)(2,1)}) %all-gather.19.cloned.1.call-update) | async-done | bytes 3145744 | tf_op jit(solution)/shard_map/all_gather | solution.py:159
  374.9 13.3 fusion.47
  388.3 97.9 %all-gather.23.cloned.1.call-done = bf16[1536,2240]{1,0:T(8,128)(2,1)} async-done(((bf16[192,2240]{1,0:T(8,128)(2,1)}), bf16[1536,2240]{1,0:T(8,128)(2,1)}) %all-gather.23.cloned.1.call-update) | async-done | bytes 6881296 | tf_op jit(solution)/shard_map/all_gather | solution.py:63
  486.2 13.2 fusion.48
  499.4 15.2 %all-gather.27.cloned.1.call-done = bf16[1024,1536]{1,0:T(8,128)(2,1)} async-done(((bf16[256,1536]{1,0:T(8,128)(2,1)}), bf16[1024,1536]{1,0:T(8,128)(2,1)}) %all-gather.27.cloned.1.call-update) | async-done | bytes 3145744 | tf_op jit(solution)/shard_map/all_gather | solution.py:177
  514.6 111.1 %all-gather.25.cloned.1.call-done = bf16[2240,1536]{0,1:T(8,128)(2,1)} async-done(((bf16[2240,192]{0,1:T(8,128)(2,1)}), bf16[2240,1536]{0,1:T(8,128)(2,1)}) %all-gather.25.cloned.1.call-update) | async-done | bytes 6881296 | tf_op jit(solution)/shard_map/all_gather | solution.py:64
  625.7 20.2 %multiply_convert_fusion = (bf16[1024,2240]{0,1:T(8,128)(2,1)}, bf16[1024,2240]{0,1:T(8,128)(2,1)}, bf16[1024,2240]{0,1:T(8,128)(2,1)}) fusion(f32[1024,2240]{0,1:T(8,128)} %fusion.47, f32[1024,2240]{0,1:T(8,128)} %fusion.48, bf16[1024,1536]{1,0:T(8,128)(2,1)} %all-gather.27.cloned.1.call-done, bf16[2240,1536]{0,1:T(8,128)(2,1)} %all-gather.25.cloned.1.call-done), kind=kOutput, calls=%fused_computation.10 | convolution fusion | flops 7080837120 | bytes 42139648 | tf_op jit(solution)/shard_map/dot_general | solution.py:16
  645.8 11.4 fusion.49
  657.3 10.1 convolution_add_fusion
  667.4 56.6 %reduce-scatter.15.cloned.1.call-done = f32[256,1536]{1,0:T(8,128)} async-done(((f32[1024,1536]{1,0:T(8,128)}), f32[256,1536]{1,0:T(8,128)}) %reduce-scatter.15.cloned.1.call-update) | async-done | bytes 1572880 | tf_op jit(solution)/shard_map/reduce_scatter | solution.py:186
  724.1 2.0 multiply_reduce_fusion
  726.1 1.4 fusion.42
  727.5 12.3 convolution_convert_fusion.2
  739.9 12.6 convolution_convert_fusion.1
  752.6 12.4 convolution_convert_fusion
  765.1 4.3 convolution_convert_fusion.6
  770.3 2.9 convolution_convert_fusion.4
  773.4 9.4 fusion.1
  782.8 1.1 bitcast_multiply_fusion
  783.9 1.6 copy-done.4
  787.9 2.9 convolution_convert_fusion.5
  791.3 9.1 fusion.45
  800.4 1.1 copy.51
  801.5 5.2 fusion.22
  806.8 2.3 fusion.43
  809.3 1.0 copy-done.16
  810.3 1.8 fusion.50
  812.1 3.6 add_convert_fusion
  816.0 12.5 convolution_convert_fusion.3
  828.6 1.1 copy-done.17
  829.8 5.4 fusion.51
  835.2 53.8 %reduce-scatter.25.cloned.1.call-done = bf16[192,2240]{1,0:T(8,128)(2,1)} async-done(((bf16[1536,2240]{1,0:T(8,128)(2,1)}), bf16[192,2240]{1,0:T(8,128)(2,1)}) %reduce-scatter.25.cloned.1.call-update) | async-done | bytes 860176 | tf_op jit(solution)/shard_map/reduce_scatter | solution.py:255
  888.9 2.5 convert_element_type.154
  891.4 129.6 %reduce-scatter.27.cloned.1.call-done = bf16[192,2240]{1,0:T(8,128)(2,1)} async-done(((bf16[1536,2240]{1,0:T(8,128)(2,1)}), bf16[192,2240]{1,0:T(8,128)(2,1)}) %reduce-scatter.27.cloned.1.call-update) | async-done | bytes 860176 | tf_op jit(solution)/shard_map/reduce_scatter | solution.py:258
  1021.0 2.5 convert_element_type.156
  1023.5 129.1 %reduce-scatter.29.cloned.1.call-done = bf16[2240,192]{0,1:T(8,128)(2,1)} async-done(((bf16[2240,1536]{0,1:T(8,128)(2,1)}), bf16[2240,192]{0,1:T(8,128)(2,1)}) %reduce-scatter.29.cloned.1.call-update) | async-done | bytes 860176 | tf_op jit(solution)/shard_map/reduce_scatter | solution.py:261
  1152.6 2.5 convert_element_type.158
  1155.6 63.8 %reduce-scatter.23.cloned.1.call-done = bf16[384,192]{0,1:T(8,128)(2,1)} async-done(((bf16[384,1536]{0,1:T(8,128)(2,1)}), bf16[384,192]{0,1:T(8,128)(2,1)}) %reduce-scatter.23.cloned.1.call-update) | async-done | bytes 147472 | tf_op jit(solution)/shard_map/reduce_scatter | solution.py:252
  1219.3 1.6 convert_element_type.152
  1221.0 65.0 %reduce-scatter.19.cloned.1.call-done = bf16[192,384]{1,0:T(8,128)(2,1)} async-done(((bf16[1536,384]{1,0:T(8,128)(2,1)}), bf16[192,384]{1,0:T(8,128)(2,1)}) %reduce-scatter.19.cloned.1.call-update) | async-done | bytes 147472 | tf_op jit(solution)/shard_map/reduce_scatter | solution.py:249
  1286.0 1.6 convert_element_type.150
  1287.6 37.9 %reduce-scatter.17.cloned.1.call-done = bf16[256,1536]{1,0:T(8,128)(2,1)} async-done(((bf16[1024,1536]{1,0:T(8,128)(2,1)}), bf16[256,1536]{1,0:T(8,128)(2,1)}) %reduce-scatter.17.cloned.1.call-update) | async-done | bytes 786448 | tf_op jit(solution)/shard_map/reduce_scatter | solution.py:233
  1325.6 1.8 fusion.16
  1327.4 39.9 %all-reduce.4 = (f32[1536]{0:T(1024)S(1)}, f32[1536]{0:T(1024)S(1)}, f32[512]{0:T(512)S(1)}, f32[1536]{0:T(1024)S(1)}) all-reduce(f32[1536]{0:T(1024)S(1)} %get-tuple-element.57, f32[1536]{0:T(1024)S(1)} %bitcast_dynamic-update-slice_fusion, ...), channel_id=6, replica_groups=mesh['dp'=8,'tensor'=4] {'dp','tensor'}, use_global_device_ids=true, to_apply=%region_14.15.clone | all-reduce | flops 5120 | bytes 40960
  1369.6 3.8 fusion.13
  1373.4 101.5 %reduce-scatter.21.cloned.1.call-done = f32[48,512]{1,0:T(8,128)} async-done(((f32[1536,512]{1,0:T(8,128)}), f32[48,512]{1,0:T(8,128)}) %reduce-scatter.21.cloned.1.call-update) | async-done | bytes 98320 | tf_op jit(solution)/shard_map/reduce_scatter | solution.py:242
  (143 shorter events, 15.5 us)
Async XLA Ops:
  7.2 5.9 copy-start.25
  7.2 76.3 %copy-start.32 = (f32[384]{0:T(512)S(1)}, f32[384]{0:T(512)}, u32[]{:S(2)}) copy-start(f32[384]{0:T(512)} %param.17) | copy-start | bytes 4612
  7.2 46.8 %all-gather.15.cloned.1.call-start = ((), (), s32[]{:S(2)}) async-start(), calls=%async_computation.12 | async-start | bytes 1327104 | tf_op jit(solution)/shard_map/all_gather | solution.py:62
  7.9 75.5 %all-gather.11.cloned.1.call-start = ((), (), s32[]{:S(2)}) async-start(), calls=%async_computation.10 | async-start | bytes 3932160 | tf_op jit(solution)/shard_map/all_gather | solution.py:130
  9.4 3.7 copy-start.26
  11.7 118.2 %all-gather.13.cloned.1.call-start = ((), (), s32[]{:S(2)}) async-start(), calls=%async_computation.11 | async-start | bytes 1769472 | tf_op jit(solution)/shard_map/all_gather | solution.py:63
  12.4 159.4 %all-gather.17.cloned.1.call-start = ((), (), s32[]{:S(2)}) async-start(), calls=%async_computation.13 | async-start | bytes 1327104 | tf_op jit(solution)/shard_map/all_gather | solution.py:64
  13.0 221.9 %reduce-scatter.11.cloned.1.call-start = ((), (), s32[]{:S(2)}) async-start(), calls=%async_computation.14 | async-start | bytes 7864320 | tf_op jit(solution)/shard_map/reduce_scatter | solution.py:155
  87.1 42.8 %copy-start.33 = (f32[512]{0:T(512)S(1)}, f32[512]{0:T(512)}, u32[]{:S(2)}) copy-start(f32[512]{0:T(512)} %param.19) | copy-start | bytes 6148
  134.1 18.1 %copy-start.22 = (f32[1024,512]{0,1:T(8,128)}, f32[1024,512]{0,1:T(8,128)S(1)}, u32[]{:S(2)}) copy-start(f32[1024,512]{0,1:T(8,128)S(1)} %convolution_add_fusion.1) | copy-start | bytes 6291460
  134.1 4.3 copy-start.7
  134.2 0.7 copy-start.8
  138.3 6.5 copy-start.18
  138.9 6.0 copy-start.20
  161.7 15.8 %copy-start.13 = (bf16[1024,3,128]{0,2,1:T(8,128)(2,1)}, bf16[1024,3,128]{0,2,1:T(8,128)(2,1)S(1)}, u32[]{:S(2)}) copy-start(bf16[1024,3,128]{0,2,1:T(8,128)(2,1)S(1)} %get-tuple-element.102) | copy-start | bytes 2359300
  177.5 57.3 %copy-start = (bf16[256,1536]{1,0:T(8,128)(2,1)S(1)}, bf16[256,1536]{1,0:T(8,128)(2,1)}, u32[]{:S(2)}) copy-start(bf16[256,1536]{1,0:T(8,128)(2,1)} %param.13) | copy-start | bytes 2359300
  177.6 59.0 %copy-start.23 = (f32[1536]{0:T(1024)S(1)}, f32[1536]{0:T(1024)}, u32[]{:S(2)}) copy-start(f32[1536]{0:T(1024)} %param.21) | copy-start | bytes 18436
  177.6 168.4 %all-gather.21.cloned.1.call-start = ((), (), s32[]{:S(2)}) async-start(), calls=%async_computation.16 | async-start | bytes 7962624 | tf_op jit(solution)/shard_map/all_gather | solution.py:62
  178.2 196.8 %all-gather.19.cloned.1.call-start = ((), (), s32[]{:S(2)}) async-start(), calls=%async_computation.15 | async-start | bytes 3932160 | tf_op jit(solution)/shard_map/all_gather | solution.py:159
  237.7 248.5 %all-gather.23.cloned.1.call-start = ((), (), s32[]{:S(2)}) async-start(), calls=%async_computation.17 | async-start | bytes 7962624 | tf_op jit(solution)/shard_map/all_gather | solution.py:63
  238.4 276.1 %all-gather.27.cloned.1.call-start = ((), (), s32[]{:S(2)}) async-start(), calls=%async_computation.20 | async-start | bytes 3932160 | tf_op jit(solution)/shard_map/all_gather | solution.py:177
  239.1 386.5 %all-gather.25.cloned.1.call-start = ((), (), s32[]{:S(2)}) async-start(), calls=%async_computation.18 | async-start | bytes 7962624 | tf_op jit(solution)/shard_map/all_gather | solution.py:64
  239.7 484.3 %reduce-scatter.15.cloned.1.call-start = ((), (), s32[]{:S(2)}) async-start(), calls=%async_computation.21 | async-start | bytes 7864320 | tf_op jit(solution)/shard_map/reduce_scatter | solution.py:186
  645.8 11.4 copy-start.28
  645.8 11.4 copy-start.34
  667.4 58.7 %copy-start.3 = (bf16[256,1536]{1,0:T(8,128)(2,1)S(1)}, bf16[256,1536]{1,0:T(8,128)(2,1)}, u32[]{:S(2)}) copy-start(bf16[256,1536]{1,0:T(8,128)(2,1)} %param.25) | copy-start | bytes 2359300
  667.4 97.7 %all-gather.29.cloned.1.call-start = ((), (), s32[]{:S(2)}) async-start(), calls=%async_computation.22 | async-start | bytes 3932160 | tf_op jit(solution)/shard_map/all_gather | solution.py:194
  724.1 2.0 copy-start.2
  727.5 161.4 %reduce-scatter.25.cloned.1.call-start = ((), (), s32[]{:S(2)}) async-start(), calls=%async_computation.27 | async-start | bytes 7962624 | tf_op jit(solution)/shard_map/reduce_scatter | solution.py:255
  739.9 281.1 %reduce-scatter.27.cloned.1.call-start = ((), (), s32[]{:S(2)}) async-start(), calls=%async_computation.28 | async-start | bytes 7962624 | tf_op jit(solution)/shard_map/reduce_scatter | solution.py:258
  752.6 400.0 %reduce-scatter.29.cloned.1.call-start = ((), (), s32[]{:S(2)}) async-start(), calls=%async_computation.29 | async-start | bytes 7962624 | tf_op jit(solution)/shard_map/reduce_scatter | solution.py:261
  765.0 454.3 %reduce-scatter.23.cloned.1.call-start = ((), (), s32[]{:S(2)}) async-start(), calls=%async_computation.26 | async-start | bytes 1327104 | tf_op jit(solution)/shard_map/reduce_scatter | solution.py:252
  765.1 4.3 copy-start.12
  765.1 5.2 copy-start.14
  765.1 5.2 copy-start.30
  769.4 0.9 copy-start.21
  773.2 512.8 %reduce-scatter.19.cloned.1.call-start = ((), (), s32[]{:S(2)}) async-start(), calls=%async_computation.24 | async-start | bytes 1327104 | tf_op jit(solution)/shard_map/reduce_scatter | solution.py:249
  773.4 9.4 copy-start.19
  782.8 2.7 copy-start.4
  785.5 1.0 copy-start.10
  785.5 1.2 copy-start.11
  785.7 2.3 copy-start.29
  787.1 0.9 copy-start.5
  790.9 534.7 %reduce-scatter.17.cloned.1.call-start = ((), (), s32[]{:S(2)}) async-start(), calls=%async_computation.23 | async-start | bytes 3932160 | tf_op jit(solution)/shard_map/reduce_scatter | solution.py:233
  801.5 5.3 copy-start.9
  806.7 3.5 copy-start.31
  809.3 1.0 copy-start.16
  810.3 1.9 copy-start.6
  810.3 1.9 copy-start.15
  815.8 553.8 %reduce-scatter.13.cloned.1.call-start = ((), (), s32[]{:S(2)}) async-start(), calls=%async_computation.19 | async-start | bytes 3932160 | tf_op jit(solution)/shard_map/reduce_scatter | solution.py:170
  828.5 1.2 copy-start.17
  828.6 646.4 %reduce-scatter.21.cloned.1.call-start = ((), (), s32[]{:S(2)}) async-start(), calls=%async_computation.25 | async-start | bytes 3244032 | tf_op jit(solution)/shard_map/reduce_scatter | solution.py:242
  891.4 434.2 %copy-start.1 = (bf16[256,1536]{1,0:T(8,128)(2,1)S(1)}, bf16[256,1536]{1,0:T(8,128)(2,1)}, u32[]{:S(2)}) copy-start(bf16[256,1536]{1,0:T(8,128)(2,1)} %param.13) | copy-start | bytes 2359300
  891.4 434.2 %copy-start.24 = (f32[1536]{0:T(1024)S(1)}, f32[1536]{0:T(1024)}, u32[]{:S(2)}) copy-start(f32[1536]{0:T(1024)} %param.15) | copy-start | bytes 18436
  891.4 434.2 %copy-start.27 = (f32[256]{0:T(256)S(1)}, f32[256]{0:T(256)}, u32[]{:S(2)}) copy-start(f32[256]{0:T(256)} %copy-done.26) | copy-start | bytes 3076
Sparse Core Ops, SparseCore 0:
  10.2 43.7 all-gather.14
  56.1 27.2 all-gather.10
  85.7 44.1 all-gather.12
  131.9 39.8 all-gather.16
  177.7 57.1 reduce-scatter.10
  237.1 108.7 all-gather.20
  348.2 26.7 all-gather.18
  377.3 108.7 all-gather.22
  487.8 26.7 all-gather.26
  516.8 108.7 all-gather.24
  667.5 56.5 reduce-scatter.14
  727.6 28.5 all-gather.28
  759.9 129.0 reduce-scatter.24
  892.9 128.0 reduce-scatter.26
  1024.5 128.0 reduce-scatter.28
  1156.2 63.0 reduce-scatter.22
  1222.9 62.9 reduce-scatter.18
  1288.5 36.9 reduce-scatter.16
  1328.1 38.3 reduce-scatter.12
  1373.2 101.6 reduce-scatter.20
where the time goes:
time: 1490 us; the launch traced here: 1480 us
  waiting for transfers between devices  1180 us (79%)
  matrix products  193 us (13%)
  other arithmetic  42.9 us (3%)
  blocking collectives  39.9 us (3%)
  between operations  15.1 us (1%)
    dot_general x18, matrix products, matmul(): return jnp.dot(left, right, preferred_element_type=jnp.float32)  152 us
    all_gather x2, waiting for transfers between devices, gather_three(): lax.all_gather(first, 'dp', axis=0, tiled=True)  146 us
    all_gather x2, waiting for transfers between devices, gather_three(): lax.all_gather(second, 'dp', axis=0, tiled=True)  140 us
    reduce_scatter x1, waiting for transfers between devices, local(): lax.psum_scatter(grad_up_w.astype(jnp.bfloat16), 'dp', scatter_dimension=...  130 us
    reduce_scatter x1, waiting for transfers between devices, local(): lax.psum_scatter(grad_down_w.astype(jnp.bfloat16), 'dp', scatter_dimensio...  129 us
    all_gather x2, waiting for transfers between devices, gather_three(): lax.all_gather(third, 'dp', axis=1, tiled=True)  121 us
    reduce_scatter x1, waiting for transfers between devices, local(): lax.psum_scatter(grad_keyval_w, ('dp', 'tensor'), scatter_dimension=0, ti...  101 us
    reduce_scatter x1, waiting for transfers between devices, local(): lax.psum_scatter(grad_query_w.astype(jnp.bfloat16), 'dp', scatter_dimensi...  65 us
  transfers between devices with their start and end apart: 20, of which 18 were waited for; matrix products, arithmetic and copies ran while one was open for 13% of the time, Pallas kernels for 0%

commit v1 on v0

--- a/solution.py
+++ b/solution.py
@@ -12,6 +12,28 @@
 masked_score = -1e30
 
 
+def in_order(pieces, dim):
+    dims = list(pieces.shape[1:])
+    dims[dim] *= pieces.shape[0]
+    return jnp.moveaxis(pieces, 0, dim).reshape(dims)
+
+
+def collect(array, axis, dim):
+    devices = lax.axis_size(axis)
+    pairs = [(i, (i + 1) % devices) for i in range(devices)]
+    back = [(b, a) for a, b in pairs]
+    lower, upper = ([], [])
+    for turn in range(devices - 1):
+        if turn % 2 == 0:
+            lower.append(lax.ppermute(lower[-1] if lower else array, axis, pairs))
+        else:
+            upper.append(lax.ppermute(upper[-1] if upper else array, axis, back))
+    parts = jnp.stack([*lower[::-1], array, *upper])
+    shift = lax.axis_index(axis) - len(lower)
+    parts = parts[(jnp.arange(devices) - shift) % devices]
+    return in_order(parts, dim)
+
+
 def matmul(left, right):
     return jnp.dot(left, right, preferred_element_type=jnp.float32)
 
@@ -61,7 +83,7 @@
     return (
         lax.all_gather(first, "dp", axis=0, tiled=True),
         lax.all_gather(second, "dp", axis=0, tiled=True),
-        lax.all_gather(third, "dp", axis=1, tiled=True),
+        collect(third, "dp", 1),
     )
 
 

time: 1490 us -> 1480 us (level)
  waiting for transfers between devices: 1180 us -> 1060 us
  starting transfers between devices: 1.6 us -> 90.7 us
  local copies, waits for them, and re-layouts: 11.4 us -> 34 us
    all_gather x2, waiting for transfers between devices: 146 us -> 6.18 us  [gather_three(): lax.all_gather(first, 'dp', axis=0, tiled=True)]
    ppermute x0 -> x14, waiting for transfers between devices: none -> 136 us  [the longest x8 121 us: collect(): lower.append(lax.ppermute(lower[-1] if lower else array, axis, pairs))]
    all_gather x2 -> x0, waiting for transfers between devices: 121 us -> none  [gather_three(): lax.all_gather(third, 'dp', axis=1, tiled=True)]
    ppermute x0 -> x14, starting transfers between devices: none -> 89.1 us  [the longest x6 77.8 us: collect(): upper.append(lax.ppermute(upper[-1] if upper else array, axis, back))]
  transfers between devices with their start and end apart: 20 -> 32, of which waited for: 18 -> 26; matrix products, arithmetic and copies ran while one was open for 13% -> 12% of each run, Pallas kernels for 0% -> 0%
where the time goes in v1:
time: 1480 us; the launch traced here: 1470 us
  waiting for transfers between devices  1060 us (72%)
  matrix products  193 us (13%)
  starting transfers between devices  90.7 us (6%)
  other arithmetic  43.8 us (3%)
  blocking collectives  39.9 us (3%)
  local copies, waits for them, and re-layouts  34 us (2%)
  between operations  15.3 us (1%)
    dot_general x18, matrix products, matmul(): return jnp.dot(left, right, preferred_element_type=jnp.float32)  153 us
    all_gather x2, waiting for transfers between devices, gather_three(): lax.all_gather(second, 'dp', axis=0, tiled=True)  140 us
    reduce_scatter x1, waiting for transfers between devices, local(): lax.psum_scatter(grad_up_w.astype(jnp.bfloat16), 'dp', scatter_dimension=...  130 us
    reduce_scatter x1, waiting for transfers between devices, local(): lax.psum_scatter(grad_down_w.astype(jnp.bfloat16), 'dp', scatter_dimensio...  129 us
    ppermute x8, waiting for transfers between devices, collect(): lower.append(lax.ppermute(lower[-1] if lower else array, axis, pairs))  121 us
    reduce_scatter x1, waiting for transfers between devices, local(): lax.psum_scatter(grad_keyval_w, ('dp', 'tensor'), scatter_dimension=0, ti...  101 us
    ppermute x6, starting transfers between devices, collect(): upper.append(lax.ppermute(upper[-1] if upper else array, axis, back))  77.8 us
    reduce_scatter x1, waiting for transfers between devices, local(): lax.psum_scatter(grad_query_w.astype(jnp.bfloat16), 'dp', scatter_dimensi...  65.1 us
  transfers between devices with their start and end apart: 32, of which 26 were waited for; matrix products, arithmetic and copies ran while one was open for 12% of the time, Pallas kernels for 0%

profile of v1, /device:TPU:0, one launch (start us, length us, event | category | flops | bytes accessed | tf_op | source)
XLA Modules:
  0.0 1474.4 jit_solution(7158856816049792713)
XLA Ops:
  9.4 2.3 fusion.18
  11.7 3.0 collective-permute-start
  14.7 3.1 collective-permute-start.4
  23.5 9.5 collective-permute-done.1
  33.1 4.8 collective-permute-start.5
  37.8 3.1 collective-permute-done.2
  42.8 5.2 collective-permute-start.6
  48.0 3.3 collective-permute-done.3
  53.7 6.2 all-gather.13.cloned.1.call-done
  59.9 29.5 %all-gather.9.cloned.1.call-done = bf16[1024,1536]{1,0:T(8,128)(2,1)} async-done(((bf16[256,1536]{1,0:T(8,128)(2,1)}), bf16[1024,1536]{1,0:T(8,128)(2,1)}) %all-gather.9.cloned.1.call-update) | async-done | bytes 3145744 | tf_op jit(solution)/shard_map/all_gather | solution.py:152
  89.4 3.6 convolution_add_fusion.2
  94.3 41.5 %all-gather.11.cloned.1.call-done = bf16[1536,512]{1,0:T(8,128)(2,1)} async-done(((bf16[192,512]{1,0:T(8,128)(2,1)}), bf16[1536,512]{1,0:T(8,128)(2,1)}) %all-gather.11.cloned.1.call-update) | async-done | bytes 1572880 | tf_op jit(solution)/shard_map/all_gather | solution.py:85
  135.8 4.2 convolution_add_fusion.1
  140.1 3.2 broadcast_multiply_fusion
  144.6 5.9 fusion.8
  150.6 7.3 exponential_reduce_fusion
  157.9 9.3 bitcast_convert_fusion
  168.2 4.5 fusion.52
  173.3 56.7 %reduce-scatter.11.cloned.1.call-done = f32[256,1536]{1,0:T(8,128)} async-done(((f32[1024,1536]{1,0:T(8,128)}), f32[256,1536]{1,0:T(8,128)}) %reduce-scatter.11.cloned.1.call-update) | async-done | bytes 1572880 | tf_op jit(solution)/shard_map/reduce_scatter | solution.py:177
  235.1 35.0 %collective-permute-done.7 = bf16[2240,192]{0,1:T(8,128)(2,1)S(1)} collective-permute-done((bf16[2240,192]{0,1:T(8,128)(2,1)S(1)}, bf16[2240,192]{0,1:T(8,128)(2,1)S(1)}, u32[]{:S(2)}, u32[]{:S(2)}) %collective-permute-start.7) | collective-permute-done | bytes 860192 | tf_op jit(solution)/shard_map/ppermute | solution.py:28
  270.1 4.7 collective-permute-start.11
  274.9 38.7 %collective-permute-done.8 = bf16[2240,192]{0,1:T(8,128)(2,1)S(1)} collective-permute-done((bf16[2240,192]{0,1:T(8,128)(2,1)S(1)}, bf16[2240,192]{0,1:T(8,128)(2,1)S(1)}, u32[]{:S(2)}, u32[]{:S(2)}) %collective-permute-start.8) | collective-permute-done | bytes 860192 | tf_op jit(solution)/shard_map/ppermute | solution.py:28
  313.6 2.5 collective-permute-start.9
  316.1 35.8 %collective-permute-start.12 = (bf16[2240,192]{0,1:T(8,128)(2,1)}, bf16[2240,192]{0,1:T(8,128)(2,1)}, u32[]{:S(2)}, u32[]{:S(2)}) collective-permute-start(bf16[2240,192]{0,1:T(8,128)(2,1)} %collective-permute-done.11), channel_id=1, source_target_pairs={{4,0},{8,4},{12,8},{16,12},{20,16},{24,20},{28,24},{0,28},{5,1},{9... | collective-permute-start | bytes 2580488 | tf_op jit(solution)/shard_map/ppermute | solution.py:30
  351.9 20.8 %collective-permute-done.9 = bf16[2240,192]{0,1:T(8,128)(2,1)} collective-permute-done((bf16[2240,192]{0,1:T(8,128)(2,1)S(1)}, bf16[2240,192]{0,1:T(8,128)(2,1)}, u32[]{:S(2)}, u32[]{:S(2)}) %collective-permute-start.9) | collective-permute-done | bytes 860192 | tf_op jit(solution)/shard_map/ppermute | solution.py:28
  372.7 2.6 collective-permute-start.10
  375.4 11.4 collective-permute-done.12
  386.8 24.1 %collective-permute-start.13 = (bf16[2240,192]{0,1:T(8,128)(2,1)}, bf16[2240,192]{0,1:T(8,128)(2,1)S(1)}, u32[]{:S(2)}, u32[]{:S(2)}) collective-permute-start(bf16[2240,192]{0,1:T(8,128)(2,1)} %collective-permute-done.12), channel_id=1, source_target_pairs={{4,0},{8,4},{12,8},{16,12},{20,16},{24,20},{28,24},{0,28},{5,1},{9... | collective-permute-start | bytes 2580488 | tf_op jit(solution)/shard_map/ppermute | solution.py:30
  410.9 9.6 collective-permute-done.10
  433.1 6.8 gather_fusion.1
  439.9 34.2 %all-gather.15.cloned.1.call-done = bf16[1024,1536]{1,0:T(8,128)(2,1)} async-done(((bf16[256,1536]{1,0:T(8,128)(2,1)}), bf16[1024,1536]{1,0:T(8,128)(2,1)}) %all-gather.15.cloned.1.call-update) | async-done | bytes 3145744 | tf_op jit(solution)/shard_map/all_gather | solution.py:181
  474.1 13.2 fusion.53
  487.3 98.1 %all-gather.19.cloned.1.call-done = bf16[1536,2240]{1,0:T(8,128)(2,1)} async-done(((bf16[192,2240]{1,0:T(8,128)(2,1)}), bf16[1536,2240]{1,0:T(8,128)(2,1)}) %all-gather.19.cloned.1.call-update) | async-done | bytes 6881296 | tf_op jit(solution)/shard_map/all_gather | solution.py:85
  585.3 13.2 fusion.54
  598.5 15.2 %all-gather.21.cloned.1.call-done = bf16[1024,1536]{1,0:T(8,128)(2,1)} async-done(((bf16[256,1536]{1,0:T(8,128)(2,1)}), bf16[1024,1536]{1,0:T(8,128)(2,1)}) %all-gather.21.cloned.1.call-update) | async-done | bytes 3145744 | tf_op jit(solution)/shard_map/all_gather | solution.py:199
  613.7 22.9 %fusion.6 = (bf16[1024,2240]{0,1:T(8,128)(2,1)}, bf16[1024,2240]{0,1:T(8,128)(2,1)}, bf16[1024,2240]{0,1:T(8,128)(2,1)}) fusion(f32[1024,2240]{0,1:T(8,128)} %fusion.53, f32[1024,2240]{0,1:T(8,128)} %fusion.54, bf16[2240,1536]{0,1:T(8,128)(2,1)} %bitcast.167, bf16[1024,1536]{1,0:T(8,128)(2,1)} %all-gather.21.cloned.1.call-done), kind=kOutput, calls=%fused_computation.17 | convolution fusion | flops 7080837120 | bytes 42139648 | tf_op jit(solution)/shard_map/dot_general | solution.py:38
  636.6 11.4 fusion.55
  648.0 9.8 convolution_add_fusion
  657.9 58.4 %reduce-scatter.15.cloned.1.call-done = f32[256,1536]{1,0:T(8,128)} async-done(((f32[1024,1536]{1,0:T(8,128)}), f32[256,1536]{1,0:T(8,128)}) %reduce-scatter.15.cloned.1.call-update) | async-done | bytes 1572880 | tf_op jit(solution)/shard_map/reduce_scatter | solution.py:208
  719.9 12.3 convolution_convert_fusion.2
  732.3 12.7 convolution_convert_fusion.1
  745.0 12.4 convolution_convert_fusion
  758.6 3.9 convolution_convert_fusion.6
  763.5 2.9 convolution_convert_fusion.4
  766.8 9.3 fusion.1
  781.2 2.9 convolution_convert_fusion.5
  784.4 9.0 fusion.51
  794.5 5.2 fusion.26
  799.8 2.3 fusion.49
  805.2 3.6 add_convert_fusion
  809.1 12.5 convolution_convert_fusion.3
  822.8 5.4 fusion.57
  828.2 53.0 %reduce-scatter.25.cloned.1.call-done = bf16[192,2240]{1,0:T(8,128)(2,1)} async-done(((bf16[1536,2240]{1,0:T(8,128)(2,1)}), bf16[192,2240]{1,0:T(8,128)(2,1)}) %reduce-scatter.25.cloned.1.call-update) | async-done | bytes 860176 | tf_op jit(solution)/shard_map/reduce_scatter | solution.py:277
  881.2 2.5 convert_element_type.154
  883.7 129.6 %reduce-scatter.27.cloned.1.call-done = bf16[192,2240]{1,0:T(8,128)(2,1)} async-done(((bf16[1536,2240]{1,0:T(8,128)(2,1)}), bf16[192,2240]{1,0:T(8,128)(2,1)}) %reduce-scatter.27.cloned.1.call-update) | async-done | bytes 860176 | tf_op jit(solution)/shard_map/reduce_scatter | solution.py:280
  1013.3 2.5 convert_element_type.156
  1015.8 129.3 %reduce-scatter.29.cloned.1.call-done = bf16[2240,192]{0,1:T(8,128)(2,1)} async-done(((bf16[2240,1536]{0,1:T(8,128)(2,1)}), bf16[2240,192]{0,1:T(8,128)(2,1)}) %reduce-scatter.29.cloned.1.call-update) | async-done | bytes 860176 | tf_op jit(solution)/shard_map/reduce_scatter | solution.py:283
  1145.1 2.5 convert_element_type.158
  1148.0 63.8 %reduce-scatter.23.cloned.1.call-done = bf16[384,192]{0,1:T(8,128)(2,1)} async-done(((bf16[384,1536]{0,1:T(8,128)(2,1)}), bf16[384,192]{0,1:T(8,128)(2,1)}) %reduce-scatter.23.cloned.1.call-update) | async-done | bytes 147472 | tf_op jit(solution)/shard_map/reduce_scatter | solution.py:274
  1213.5 65.1 %reduce-scatter.19.cloned.1.call-done = bf16[192,384]{1,0:T(8,128)(2,1)} async-done(((bf16[1536,384]{1,0:T(8,128)(2,1)}), bf16[192,384]{1,0:T(8,128)(2,1)}) %reduce-scatter.19.cloned.1.call-update) | async-done | bytes 147472 | tf_op jit(solution)/shard_map/reduce_scatter | solution.py:271
  1280.2 37.9 %reduce-scatter.17.cloned.1.call-done = bf16[256,1536]{1,0:T(8,128)(2,1)} async-done(((bf16[1024,1536]{1,0:T(8,128)(2,1)}), bf16[256,1536]{1,0:T(8,128)(2,1)}) %reduce-scatter.17.cloned.1.call-update) | async-done | bytes 786448 | tf_op jit(solution)/shard_map/reduce_scatter | solution.py:255
  1319.9 39.9 %all-reduce.4 = (f32[1536]{0:T(1024)S(1)}, f32[1536]{0:T(1024)S(1)}, f32[512]{0:T(512)S(1)}, f32[1536]{0:T(1024)S(1)}) all-reduce(f32[1536]{0:T(1024)S(1)} %get-tuple-element.57, f32[1536]{0:T(1024)S(1)} %bitcast_dynamic-update-slice_fusion.16, ...), channel_id=6, replica_groups=mesh['dp'=8,'tensor'=4] {'dp','tensor'}, use_global_device_ids=true, to_apply=%region_14.15.clone | all-reduce | flops 5120 | bytes 40960
  1362.2 3.8 fusion.17
  1366.0 101.3 %reduce-scatter.21.cloned.1.call-done = f32[48,512]{1,0:T(8,128)} async-done(((f32[1536,512]{1,0:T(8,128)}), f32[48,512]{1,0:T(8,128)}) %reduce-scatter.21.cloned.1.call-update) | async-done | bytes 98320 | tf_op jit(solution)/shard_map/reduce_scatter | solution.py:264
  (219 shorter events, 59.2 us)
Async XLA Ops:
  7.2 4.5 copy-start.33
  7.2 10.7 copy-start.36
  7.2 52.7 %all-gather.13.cloned.1.call-start = ((), (), s32[]{:S(2)}) async-start(), calls=%async_computation.12 | async-start | bytes 1327104 | tf_op jit(solution)/shard_map/all_gather | solution.py:84
  7.9 81.5 %all-gather.9.cloned.1.call-start = ((), (), s32[]{:S(2)}) async-start(), calls=%async_computation.10 | async-start | bytes 3932160 | tf_op jit(solution)/shard_map/all_gather | solution.py:152
  11.7 124.2 %all-gather.11.cloned.1.call-start = ((), (), s32[]{:S(2)}) async-start(), calls=%async_computation.11 | async-start | bytes 1769472 | tf_op jit(solution)/shard_map/all_gather | solution.py:85
  11.7 10.0 collective-permute-start
  14.7 18.3 %collective-permute-start.4 = (bf16[384,192]{0,1:T(8,128)(2,1)S(1)}, bf16[384,192]{0,1:T(8,128)(2,1)S(1)}, u32[]{:S(2)}, u32[]{:S(2)}) collective-permute-start(bf16[384,192]{0,1:T(8,128)(2,1)S(1)} %copy-done.33), channel_id=1, source_target_pairs={{4,0},{8,4},{12,8},{16,12},{20,16},{24,20},{28,24},{0,28},{5,1},{9... | collective-permute-start | bytes 442376 | tf_op jit(solution)/shard_map/ppermute | solution.py:30
  17.9 212.1 %reduce-scatter.11.cloned.1.call-start = ((), (), s32[]{:S(2)}) async-start(), calls=%async_computation.13 | async-start | bytes 7864320 | tf_op jit(solution)/shard_map/reduce_scatter | solution.py:177
  18.0 71.4 %copy-start.49 = (f32[384]{0:T(512)S(1)}, f32[384]{0:T(512)}, u32[]{:S(2)}) copy-start(f32[384]{0:T(512)} %param.17) | copy-start | bytes 4612
  21.7 11.2 collective-permute-start.1
  32.9 7.9 collective-permute-start.2
  33.1 9.7 collective-permute-start.5
  40.9 10.4 collective-permute-start.3
  42.8 10.1 collective-permute-start.6
  53.7 113.6 %copy-start.4 = (bf16[8,384,192]{1,2,0:T(8,128)(2,1)}, bf16[8,384,192]{1,2,0:T(8,128)(2,1)S(1)}, u32[]{:S(2)}) copy-start(bf16[8,384,192]{1,2,0:T(8,128)(2,1)S(1)} %gather_fusion) | copy-start | bytes 3538948
  93.0 42.8 %copy-start.50 = (f32[512]{0:T(512)S(1)}, f32[512]{0:T(512)}, u32[]{:S(2)}) copy-start(f32[512]{0:T(512)} %param.19) | copy-start | bytes 6148
  140.0 17.9 %copy-start.32 = (f32[1024,512]{0,1:T(8,128)}, f32[1024,512]{0,1:T(8,128)S(1)}, u32[]{:S(2)}) copy-start(f32[1024,512]{0,1:T(8,128)S(1)} %convolution_add_fusion.1) | copy-start | bytes 6291460
  140.1 3.7 copy-start.13
  143.3 7.3 copy-start.23
  143.8 6.7 copy-start.30
  157.9 9.4 copy-start.39
  172.6 57.4 %copy-start = (bf16[256,1536]{1,0:T(8,128)(2,1)S(1)}, bf16[256,1536]{1,0:T(8,128)(2,1)}, u32[]{:S(2)}) copy-start(bf16[256,1536]{1,0:T(8,128)(2,1)} %param.13) | copy-start | bytes 2359300
  172.6 59.1 %copy-start.34 = (f32[1536]{0:T(1024)S(1)}, f32[1536]{0:T(1024)}, u32[]{:S(2)}) copy-start(f32[1536]{0:T(1024)} %param.21) | copy-start | bytes 18436
  172.7 267.2 %all-gather.17.cloned.1.call-start = ((), (), s32[]{:S(2)}) async-start(), calls=%async_computation.15 | async-start | bytes 7962624 | tf_op jit(solution)/shard_map/all_gather | solution.py:84
  173.3 60.4 %copy-start.25 = (bf16[2240,192]{0,1:T(8,128)(2,1)S(1)}, bf16[2240,192]{0,1:T(8,128)(2,1)}, u32[]{:S(2)}) copy-start(bf16[2240,192]{0,1:T(8,128)(2,1)} %param.24) | copy-start | bytes 2580484
  173.3 300.8 %all-gather.15.cloned.1.call-start = ((), (), s32[]{:S(2)}) async-start(), calls=%async_computation.14 | async-start | bytes 3932160 | tf_op jit(solution)/shard_map/all_gather | solution.py:181
  231.7 486.7 %copy-start.37 = (f32[256]{0:T(256)}, f32[256]{0:T(256)S(1)}, u32[]{:S(2)}) copy-start(f32[256]{0:T(256)S(1)} %add_rsqrt_fusion) | copy-start | bytes 3076
  232.8 352.5 %all-gather.19.cloned.1.call-start = ((), (), s32[]{:S(2)}) async-start(), calls=%async_computation.16 | async-start | bytes 7962624 | tf_op jit(solution)/shard_map/all_gather | solution.py:85
  233.6 380.1 %all-gather.21.cloned.1.call-start = ((), (), s32[]{:S(2)}) async-start(), calls=%async_computation.18 | async-start | bytes 3932160 | tf_op jit(solution)/shard_map/all_gather | solution.py:199
  233.6 36.5 %collective-permute-start.7 = (bf16[2240,192]{0,1:T(8,128)(2,1)S(1)}, bf16[2240,192]{0,1:T(8,128)(2,1)S(1)}, u32[]{:S(2)}, u32[]{:S(2)}) collective-permute-start(bf16[2240,192]{0,1:T(8,128)(2,1)S(1)} %copy-done.25), channel_id=1, source_target_pairs={{0,4},{4,8},{8,12},{12,16},{16,20},{20,24},{24,28},{28,0},{1,5},{5... | collective-permute-start | bytes 2580488 | tf_op jit(solution)/shard_map/ppermute | solution.py:28
  270.1 45.9 %copy-start.26 = (bf16[2240,192]{0,1:T(8,128)(2,1)}, bf16[2240,192]{0,1:T(8,128)(2,1)S(1)}, u32[]{:S(2)}) copy-start(bf16[2240,192]{0,1:T(8,128)(2,1)S(1)} %collective-permute-done.7) | copy-start | bytes 2580484
  270.1 43.5 %collective-permute-start.8 = (bf16[2240,192]{0,1:T(8,128)(2,1)S(1)}, bf16[2240,192]{0,1:T(8,128)(2,1)S(1)}, u32[]{:S(2)}, u32[]{:S(2)}) collective-permute-start(bf16[2240,192]{0,1:T(8,128)(2,1)S(1)} %collective-permute-done.7), channel_id=1, source_target_pairs={{0,4},{4,8},{8,12},{12,16},{16,20},{20,24},{24,28},{28,0},{1,5},{5... | collective-permute-start | bytes 2580488 | tf_op jit(solution)/shard_map/ppermute | solution.py:28
  270.1 45.9 %collective-permute-start.11 = (bf16[2240,192]{0,1:T(8,128)(2,1)S(1)}, bf16[2240,192]{0,1:T(8,128)(2,1)}, u32[]{:S(2)}, u32[]{:S(2)}) collective-permute-start(bf16[2240,192]{0,1:T(8,128)(2,1)S(1)} %copy-done.25), channel_id=1, source_target_pairs={{4,0},{8,4},{12,8},{16,12},{20,16},{24,20},{28,24},{0,28},{5,1},{9... | collective-permute-start | bytes 2580488 | tf_op jit(solution)/shard_map/ppermute | solution.py:30
  313.6 38.3 %copy-start.28 = (bf16[2240,192]{0,1:T(8,128)(2,1)}, bf16[2240,192]{0,1:T(8,128)(2,1)S(1)}, u32[]{:S(2)}) copy-start(bf16[2240,192]{0,1:T(8,128)(2,1)S(1)} %collective-permute-done.8) | copy-start | bytes 2580484
  313.6 59.1 %collective-permute-start.9 = (bf16[2240,192]{0,1:T(8,128)(2,1)S(1)}, bf16[2240,192]{0,1:T(8,128)(2,1)}, u32[]{:S(2)}, u32[]{:S(2)}) collective-permute-start(bf16[2240,192]{0,1:T(8,128)(2,1)S(1)} %collective-permute-done.8), channel_id=1, source_target_pairs={{0,4},{4,8},{8,12},{12,16},{16,20},{20,24},{24,28},{28,0},{1,5},{5... | collective-permute-start | bytes 2580488 | tf_op jit(solution)/shard_map/ppermute | solution.py:28
  316.1 70.7 %collective-permute-start.12 = (bf16[2240,192]{0,1:T(8,128)(2,1)}, bf16[2240,192]{0,1:T(8,128)(2,1)}, u32[]{:S(2)}, u32[]{:S(2)}) collective-permute-start(bf16[2240,192]{0,1:T(8,128)(2,1)} %collective-permute-done.11), channel_id=1, source_target_pairs={{4,0},{8,4},{12,8},{16,12},{20,16},{24,20},{28,24},{0,28},{5,1},{9... | collective-permute-start | bytes 2580488 | tf_op jit(solution)/shard_map/ppermute | solution.py:30
  372.7 47.7 %collective-permute-start.10 = (bf16[2240,192]{0,1:T(8,128)(2,1)}, bf16[2240,192]{0,1:T(8,128)(2,1)}, u32[]{:S(2)}, u32[]{:S(2)}) collective-permute-start(bf16[2240,192]{0,1:T(8,128)(2,1)} %collective-permute-done.9), channel_id=1, source_target_pairs={{0,4},{4,8},{8,12},{12,16},{16,20},{20,24},{24,28},{28,0},{1,5},{5... | collective-permute-start | bytes 2580488 | tf_op jit(solution)/shard_map/ppermute | solution.py:28
  375.3 341.1 %reduce-scatter.15.cloned.1.call-start = ((), (), s32[]{:S(2)}) async-start(), calls=%async_computation.19 | async-start | bytes 7864320 | tf_op jit(solution)/shard_map/reduce_scatter | solution.py:208
  375.3 49.4 %copy-start.29 = (bf16[2240,192]{0,1:T(8,128)(2,1)S(1)}, bf16[2240,192]{0,1:T(8,128)(2,1)}, u32[]{:S(2)}) copy-start(bf16[2240,192]{0,1:T(8,128)(2,1)} %copy-done.28) | copy-start | bytes 2580484
  375.4 50.4 %copy-start.27 = (bf16[2240,192]{0,1:T(8,128)(2,1)S(1)}, bf16[2240,192]{0,1:T(8,128)(2,1)}, u32[]{:S(2)}) copy-start(bf16[2240,192]{0,1:T(8,128)(2,1)} %copy-done.26) | copy-start | bytes 2580484
  386.8 45.3 %collective-permute-start.13 = (bf16[2240,192]{0,1:T(8,128)(2,1)}, bf16[2240,192]{0,1:T(8,128)(2,1)S(1)}, u32[]{:S(2)}, u32[]{:S(2)}) collective-permute-start(bf16[2240,192]{0,1:T(8,128)(2,1)} %collective-permute-done.12), channel_id=1, source_target_pairs={{4,0},{8,4},{12,8},{16,12},{20,16},{24,20},{28,24},{0,28},{5,1},{9... | collective-permute-start | bytes 2580488 | tf_op jit(solution)/shard_map/ppermute | solution.py:30
  636.6 11.4 copy-start.45
  636.6 11.4 copy-start.51
  657.9 60.5 %copy-start.3 = (bf16[256,1536]{1,0:T(8,128)(2,1)S(1)}, bf16[256,1536]{1,0:T(8,128)(2,1)}, u32[]{:S(2)}) copy-start(bf16[256,1536]{1,0:T(8,128)(2,1)} %param.25) | copy-start | bytes 2359300
  657.9 99.5 %all-gather.23.cloned.1.call-start = ((), (), s32[]{:S(2)}) async-start(), calls=%async_computation.20 | async-start | bytes 3932160 | tf_op jit(solution)/shard_map/all_gather | solution.py:216
  718.4 13.8 copy-start.43
  719.8 161.4 %reduce-scatter.25.cloned.1.call-start = ((), (), s32[]{:S(2)}) async-start(), calls=%async_computation.25 | async-start | bytes 7962624 | tf_op jit(solution)/shard_map/reduce_scatter | solution.py:277
  732.2 281.1 %reduce-scatter.27.cloned.1.call-start = ((), (), s32[]{:S(2)}) async-start(), calls=%async_computation.26 | async-start | bytes 7962624 | tf_op jit(solution)/shard_map/reduce_scatter | solution.py:280
  744.9 400.1 %reduce-scatter.29.cloned.1.call-start = ((), (), s32[]{:S(2)}) async-start(), calls=%async_computation.27 | async-start | bytes 7962624 | tf_op jit(solution)/shard_map/reduce_scatter | solution.py:283
  757.4 454.5 %reduce-scatter.23.cloned.1.call-start = ((), (), s32[]{:S(2)}) async-start(), calls=%async_computation.24 | async-start | bytes 1327104 | tf_op jit(solution)/shard_map/reduce_scatter | solution.py:274
  758.6 4.0 copy-start.17
  758.6 4.8 copy-start.19
  758.6 4.8 copy-start.47
  766.3 512.2 %reduce-scatter.19.cloned.1.call-start = ((), (), s32[]{:S(2)}) async-start(), calls=%async_computation.22 | async-start | bytes 1327104 | tf_op jit(solution)/shard_map/reduce_scatter | solution.py:271
  766.8 9.3 copy-start.24
  784.2 533.9 %reduce-scatter.17.cloned.1.call-start = ((), (), s32[]{:S(2)}) async-start(), calls=%async_computation.21 | async-start | bytes 3932160 | tf_op jit(solution)/shard_map/reduce_scatter | solution.py:255
  794.5 5.3 copy-start.14
  808.8 553.3 %reduce-scatter.13.cloned.1.call-start = ((), (), s32[]{:S(2)}) async-start(), calls=%async_computation.17 | async-start | bytes 3932160 | tf_op jit(solution)/shard_map/reduce_scatter | solution.py:192
  821.6 645.7 %reduce-scatter.21.cloned.1.call-start = ((), (), s32[]{:S(2)}) async-start(), calls=%async_computation.23 | async-start | bytes 3244032 | tf_op jit(solution)/shard_map/reduce_scatter | solution.py:264
  883.7 434.4 %copy-start.1 = (bf16[256,1536]{1,0:T(8,128)(2,1)S(1)}, bf16[256,1536]{1,0:T(8,128)(2,1)}, u32[]{:S(2)}) copy-start(bf16[256,1536]{1,0:T(8,128)(2,1)} %param.13) | copy-start | bytes 2359300
  883.7 434.4 %copy-start.35 = (f32[1536]{0:T(1024)S(1)}, f32[1536]{0:T(1024)}, u32[]{:S(2)}) copy-start(f32[1536]{0:T(1024)} %param.15) | copy-start | bytes 18436
  883.7 434.4 %copy-start.42 = (f32[256]{0:T(256)S(1)}, f32[256]{0:T(256)}, u32[]{:S(2)}) copy-start(f32[256]{0:T(256)} %copy-done.41) | copy-start | bytes 3076
  1015.8 346.3 %copy-start.38 = (f32[256]{0:T(256)S(1)}, f32[256]{0:T(256)}, u32[]{:S(2)}) copy-start(f32[256]{0:T(256)} %copy-done.37) | copy-start | bytes 3076
  1015.8 346.3 %copy-start.44 = (f32[256]{0:T(256)S(1)}, f32[256]{0:T(256)}, u32[]{:S(2)}) copy-start(f32[256]{0:T(256)} %copy-done.43) | copy-start | bytes 3076
  (20 other events, 39.5 us)
Sparse Core Ops, SparseCore 0:
  10.2 49.6 all-gather.12
  62.0 27.3 all-gather.8
  91.6 44.1 all-gather.10
  172.8 57.1 reduce-scatter.10
  232.3 204.5 all-gather.16
  438.9 35.1 all-gather.14
  476.5 108.7 all-gather.18
  587.0 26.7 all-gather.20
  658.0 58.3 reduce-scatter.14
  719.9 28.5 all-gather.22
  752.2 128.9 reduce-scatter.24
  885.2 128.0 reduce-scatter.26
  1017.0 128.0 reduce-scatter.28
  1148.7 63.1 reduce-scatter.22
  1215.5 63.0 reduce-scatter.18
  1281.1 36.9 reduce-scatter.16
  1320.5 38.2 reduce-scatter.12
  1365.6 101.7 reduce-scatter.20
